TPU v7x, 128 devices: a whole 4x4x4 slice. The times are simulated.
128 devices in a mesh: req: 64 (over z_lo, x, y, core), kvh: 2 (over z_hi).
Axes of the slice: x: 4, y: 4, z: 4 (z_hi: 2, z_lo: 2; z = z_hi * 2 + z_lo), core: 2. Of those that a mesh axis runs over, the one named last changes fastest.
Arguments:
- queries: bfloat16 [64, 4, 8192], P('req', None, 'kvh'), may hold values from -42 to 42
- incoming_keys: bfloat16 [64, 4, 1024], P('req', None, 'kvh'), may hold values from -6 to 6
- incoming_values: bfloat16 [64, 4, 1024], P('req', None, 'kvh'), may hold values from -6 to 6
- system_prefix_keys: bfloat16 [8, 16384, 1024], P(None, 'req', 'kvh'), may hold values from -6 to 6
- system_prefix_values: bfloat16 [8, 16384, 1024], P(None, 'req', 'kvh'), may hold values from -6 to 6
- request_history_keys: bfloat16 [64, 2048, 1024], P('req', None, 'kvh'), may hold values from -6 to 6
- request_history_values: bfloat16 [64, 2048, 1024], P('req', None, 'kvh'), may hold values from -6 to 6
- kept: int32 [64, 8, 1024], P('req', 'kvh'), may hold values from 0 to 2047, as said below
- membership: int32 [64, 1], P('req'), may hold values from 0 to 7; in each aligned block of 64 rows (0 to 63, 64 to 127, ...) at most 16 rows name the same one
- out_weight: bfloat16 [8192, 8192], P('kvh', 'req'), may hold values from -0.0625 to 0.0625
Outputs:
- layer_out: bfloat16 [64, 4, 8192], P(None, None, 'req')
Inputs may be any that keep to these rules, and one draw needn't show every extreme that they name: `membership`: no system prompt has more than 16 requests; some prompt has exactly 16. `kept`: the 1024 positions of one request and KV head are distinct.
All inputs are finite; a program needn't handle non-finite values.
Results may differ from a plain program's by a relative error of at most 0.0049.
Values may be sent and summed in bfloat16 or wider, within the bound.
No kernel may reach another device: no remote copies, remote signals or barrier semaphores. Data moves between devices by JAX's collectives and lax.ppermute only.
A program may use at most 128 MiB of HBM per device.

v0:
```python
import jax
import jax.numpy as jnp
from jax import lax
from jax.sharding import PartitionSpec as P

HEAD_WIDTH = 128
HEADS_PER_GROUP = 8
PROMPT_COUNT = 8


def local_partial(scores):
    row_peak = jnp.max(scores, axis=-1)
    exp_terms = jnp.exp(scores - row_peak[..., None])
    row_total = jnp.sum(exp_terms, axis=-1)
    return (row_peak, row_total, exp_terms.astype(jnp.bfloat16))


def prefix_partials(
    query_all, member_all, system_prefix_keys, system_prefix_values, kv_local, score_scale
):
    total_rows, span_steps = (query_all.shape[0], query_all.shape[1])
    capacity = total_rows // 4
    stretch_len = system_prefix_keys.shape[1]
    member_ids = member_all[:, 0]
    onehot_table = member_ids[:, None] == jnp.arange(PROMPT_COUNT)[None, :]
    prompt_counts = jnp.sum(onehot_table.astype(jnp.int32), axis=0)
    prompt_starts = jnp.cumsum(prompt_counts) - prompt_counts
    sorted_order = jnp.argsort(member_ids, stable=True)
    grouped_query_heads = query_all.reshape(
        total_rows, span_steps, kv_local, HEADS_PER_GROUP, HEAD_WIDTH
    )
    peak_all = jnp.zeros((total_rows, span_steps, kv_local, HEADS_PER_GROUP), jnp.float32)
    total_all = jnp.zeros((total_rows, span_steps, kv_local, HEADS_PER_GROUP), jnp.float32)
    out_all = jnp.zeros(
        (total_rows, span_steps, kv_local, HEADS_PER_GROUP, HEAD_WIDTH), jnp.float32
    )
    slot_ids = jnp.arange(capacity)
    for prompt_id in range(PROMPT_COUNT):
        slot_pos = jnp.minimum(prompt_starts[prompt_id] + slot_ids, total_rows - 1)
        slot_rows = sorted_order[slot_pos]
        is_valid = (slot_ids < prompt_counts[prompt_id])[:, None, None, None]
        chosen_index = grouped_query_heads[slot_rows]
        stretch_keys = system_prefix_keys[prompt_id].reshape(stretch_len, kv_local, HEAD_WIDTH)
        stretch_values = system_prefix_values[prompt_id].reshape(stretch_len, kv_local, HEAD_WIDTH)
        scores = (
            jnp.einsum(
                "cskgd,lkd->cskgl", chosen_index, stretch_keys, preferred_element_type=jnp.float32
            )
            * score_scale
        )
        row_peak, row_total, weights = local_partial(scores)
        part_out = jnp.einsum(
            "cskgl,lkd->cskgd", weights, stretch_values, preferred_element_type=jnp.float32
        )
        peak_all = peak_all.at[slot_rows].add(jnp.where(is_valid, row_peak, 0.0))
        total_all = total_all.at[slot_rows].add(jnp.where(is_valid, row_total, 0.0))
        out_all = out_all.at[slot_rows].add(jnp.where(is_valid[..., None], part_out, 0.0))
    return (peak_all, total_all, out_all)


def return_partials(peak_all, total_all, out_all, req_rows):
    total_rows, span_steps, kv_local = (peak_all.shape[0], peak_all.shape[1], peak_all.shape[2])
    flat_peak = peak_all.reshape(total_rows, span_steps, kv_local * HEADS_PER_GROUP)
    flat_total = total_all.reshape(total_rows, span_steps, kv_local * HEADS_PER_GROUP)
    flat_out = out_all.reshape(total_rows, span_steps, kv_local * HEADS_PER_GROUP * HEAD_WIDTH)
    got_out, got_peak, got_total = (
        lax.all_to_all(flat_out, "req", split_axis=0, concat_axis=0, tiled=True),
        lax.all_to_all(flat_peak, "req", split_axis=0, concat_axis=0, tiled=True),
        lax.all_to_all(flat_total, "req", split_axis=0, concat_axis=0, tiled=True),
    )
    sources = total_rows // req_rows
    return (
        got_peak.reshape(sources, req_rows, span_steps, kv_local, HEADS_PER_GROUP),
        got_total.reshape(sources, req_rows, span_steps, kv_local, HEADS_PER_GROUP),
        got_out.reshape(sources, req_rows, span_steps, kv_local, HEADS_PER_GROUP, HEAD_WIDTH),
    )


def local(
    queries,
    incoming_keys,
    incoming_values,
    system_prefix_keys,
    system_prefix_values,
    request_history_keys,
    request_history_values,
    kept,
    membership,
    out_weight,
):
    req_rows, step_count, query_width = queries.shape
    kv_local = incoming_keys.shape[2] // HEAD_WIDTH
    score_scale = HEAD_WIDTH ** (-0.5)
    grouped_query_heads = queries.reshape(
        req_rows, step_count, kv_local, HEADS_PER_GROUP, HEAD_WIDTH
    )
    cache_keys = request_history_keys.reshape(req_rows, -1, kv_local, HEAD_WIDTH)
    cache_values = request_history_values.reshape(req_rows, -1, kv_local, HEAD_WIDTH)
    head_index_list = jnp.arange(kv_local)[None, :]
    retained_keys = jax.vmap(lambda key_table, pick_list: key_table[pick_list.T, head_index_list])(
        cache_keys, kept
    )
    retained_values = jax.vmap(
        lambda value_table, pick_list: value_table[pick_list.T, head_index_list]
    )(cache_values, kept)
    kept_scores = (
        jnp.einsum(
            "rtkgd,rlkd->rtkgl",
            grouped_query_heads,
            retained_keys,
            preferred_element_type=jnp.float32,
        )
        * score_scale
    )
    kept_peak, kept_total, kept_weights = local_partial(kept_scores)
    kept_out = jnp.einsum(
        "rtkgl,rlkd->rtkgd", kept_weights, retained_values, preferred_element_type=jnp.float32
    )
    recent_token_keys = incoming_keys.reshape(req_rows, step_count, kv_local, HEAD_WIDTH)
    recent_token_values = incoming_values.reshape(req_rows, step_count, kv_local, HEAD_WIDTH)
    fresh_scores = (
        jnp.einsum(
            "rtkgd,rukd->rtkgu",
            grouped_query_heads,
            recent_token_keys,
            preferred_element_type=jnp.float32,
        )
        * score_scale
    )
    causal_mask = jnp.arange(step_count)[None, :] <= jnp.arange(step_count)[:, None]
    fresh_scores = jnp.where(causal_mask[None, :, None, None, :], fresh_scores, -1e30)
    recent_score_peak, recent_weight_sum, fresh_weights = local_partial(fresh_scores)
    recent_output = jnp.einsum(
        "rtkgu,rukd->rtkgd", fresh_weights, recent_token_values, preferred_element_type=jnp.float32
    )
    partial_sets = []
    for step_index in range(step_count):
        query_all, member_all = (
            lax.all_gather(queries[:, step_index : step_index + 1], "req", axis=0, tiled=True),
            lax.all_gather(membership, "req", axis=0, tiled=True),
        )
        partial_sets.append(
            return_partials(
                *prefix_partials(
                    query_all,
                    member_all,
                    system_prefix_keys,
                    system_prefix_values,
                    kv_local,
                    score_scale,
                ),
                req_rows
            )
        )
    src_peak = jnp.concatenate([entry[0] for entry in partial_sets], axis=2)
    src_total = jnp.concatenate([entry[1] for entry in partial_sets], axis=2)
    src_out = jnp.concatenate([entry[2] for entry in partial_sets], axis=2)
    top_score = jnp.maximum(jnp.maximum(jnp.max(src_peak, axis=0), kept_peak), recent_score_peak)
    src_factor = jnp.exp(src_peak - top_score[None])
    kept_factor = jnp.exp(kept_peak - top_score)
    fresh_factor = jnp.exp(recent_score_peak - top_score)
    numerator = (
        jnp.sum(src_factor[..., None] * src_out, axis=0)
        + kept_factor[..., None] * kept_out
        + fresh_factor[..., None] * recent_output
    )
    denominator = (
        jnp.sum(src_factor * src_total, axis=0)
        + kept_factor * kept_total
        + fresh_factor * recent_weight_sum
    )
    attention = (
        (numerator / denominator[..., None])
        .astype(jnp.bfloat16)
        .reshape(req_rows, step_count, query_width)
    )
    piece_rows = lax.all_gather(attention, "req", axis=0, tiled=True)
    flat_rows = piece_rows.reshape(-1, query_width)
    partial_out = jnp.dot(flat_rows, out_weight, preferred_element_type=jnp.float32).reshape(
        piece_rows.shape[0], step_count, -1
    )
    return lax.psum(partial_out, "kvh").astype(jnp.bfloat16)


def solution(mesh):
    placed = (
        P("req", None, "kvh"),
        P("req", None, "kvh"),
        P("req", None, "kvh"),
        P(None, "req", "kvh"),
        P(None, "req", "kvh"),
        P("req", None, "kvh"),
        P("req", None, "kvh"),
        P("req", "kvh", None),
        P("req", None),
        P("kvh", "req"),
    )
    return jax.shard_map(
        local, mesh=mesh, in_specs=placed, out_specs=P(None, None, "req"), check_vma=False
    )
```

profile of v0, /device:TPU:0, one launch (start us, length us, event | category | flops | bytes accessed | tf_op | source)
XLA Modules:
  0.0 1125.0 jit_solution(11656335214572381754)
XLA Ops:
  9.2 20.6 %all-reduce = s32[64]{0:T(128)S(1)} all-reduce(s32[64]{0:T(128)S(1)} %bitcast_dynamic-update-slice_fusion), channel_id=1, replica_groups=mesh['req'=64,'kvh'=2] {'req'}, use_global_device_ids=true, to_apply=%add | all-reduce | flops 64 | bytes 512 | tf_op jit(solution)/shard_map/squeeze | solution.py:24
  35.8 79.2 %all_gather.22 = bf16[64,1,4096]{2,1,0:T(2,128)(2,1)S(1)} all-gather(bf16[1,1,4096]{2,1,0:T(2,128)(2,1)S(1)} %get-tuple-element.26), channel_id=1, replica_groups=mesh['req'=64,'kvh'=2] {'req'}, dimensions={0}, use_global_device_ids=true | all-gather | bytes 532480 | tf_op jit(solution)/shard_map/all_gather | solution.py:139
  115.0 3.3 reduce.71
  118.4 80.7 %all_gather.23 = bf16[64,1,4096]{2,1,0:T(2,128)(2,1)S(1)} all-gather(bf16[1,1,4096]{2,1,0:T(2,128)(2,1)S(1)} %get-tuple-element.28), channel_id=1, replica_groups=mesh['req'=64,'kvh'=2] {'req'}, dimensions={0}, use_global_device_ids=true | all-gather | bytes 532480 | tf_op jit(solution)/shard_map/all_gather | solution.py:139
  199.1 3.3 reduce.72
  208.0 79.4 %all_gather.24 = bf16[64,1,4096]{2,1,0:T(2,128)(2,1)S(1)} all-gather(bf16[1,1,4096]{2,1,0:T(2,128)(2,1)S(1)} %get-tuple-element.27), channel_id=1, replica_groups=mesh['req'=64,'kvh'=2] {'req'}, dimensions={0}, use_global_device_ids=true | all-gather | bytes 532480 | tf_op jit(solution)/shard_map/all_gather | solution.py:139
  287.4 4.1 reduce.73
  295.1 85.8 %all_gather.25 = bf16[64,1,4096]{2,1,0:T(2,128)(2,1)} all-gather(bf16[1,1,4096]{2,1,0:T(2,128)(2,1)S(1)} %get-tuple-element.29), channel_id=1, replica_groups=mesh['req'=64,'kvh'=2] {'req'}, dimensions={0}, use_global_device_ids=true | all-gather | bytes 532480 | tf_op jit(solution)/shard_map/all_gather | solution.py:139
  380.8 5.1 reduce.74
  426.1 2.7 fusion.409
  502.6 5.6 all-to-all-start.11
  508.2 2.9 fusion.408
  532.0 2.2 fusion.93
  553.3 9.4 all-to-all-start.10
  585.0 9.3 all-to-all-start.9
  613.1 9.6 all-to-all-start.8
  640.6 9.3 all-to-all-start.3
  668.7 9.4 all-to-all-start.2
  690.9 9.0 all-to-all-start.1
  713.5 9.1 all-to-all-start
  728.5 2.4 scatter_fusion.56
  731.0 2.4 scatter_fusion.57
  733.4 2.4 scatter_fusion.58
  735.8 2.4 scatter_fusion.59
  738.3 2.4 scatter_fusion.60
  740.7 2.4 scatter_fusion.61
  743.1 2.4 scatter_fusion.62
  745.6 2.6 scatter_fusion.63
  748.2 9.7 all-to-all-start.7
  761.2 2.4 scatter_fusion.48
  763.6 2.4 scatter_fusion.49
  766.1 2.4 scatter_fusion.50
  768.5 2.4 scatter_fusion.51
  770.9 2.4 scatter_fusion.52
  773.3 2.4 scatter_fusion.53
  775.8 2.4 scatter_fusion.54
  778.3 2.6 scatter_fusion.55
  787.2 9.9 all-to-all-start.6
  799.4 2.4 scatter_fusion.40
  801.8 2.4 scatter_fusion.41
  804.3 2.4 scatter_fusion.42
  806.7 2.4 scatter_fusion.43
  809.1 2.4 scatter_fusion.44
  811.6 2.4 scatter_fusion.45
  814.0 2.4 scatter_fusion.46
  816.5 2.6 scatter_fusion.47
  823.7 9.5 all-to-all-start.5
  834.2 4.0 reshape.1933
  843.5 66.3 %gather_fusion.40 = bf16[4096,128]{1,0:T(8,128)(2,1)} fusion(bf16[1,2048,4,128]{3,2,1,0:T(4,128)(2,1)} %reshape.1933, s32[4096]{0:T(1024)S(1)} %reshape.2369), kind=kCustom, calls=%fused_computation.40 | custom fusion | bytes 2146304 | tf_op jit(solution)/shard_map/vmap()/gather | solution.py:100
  910.9 2.4 scatter_fusion.32
  913.3 2.4 scatter_fusion.33
  915.8 2.4 scatter_fusion.34
  918.2 2.4 scatter_fusion.35
  920.6 2.4 scatter_fusion.36
  923.0 2.4 scatter_fusion.37
  925.5 2.4 scatter_fusion.38
  927.9 2.6 scatter_fusion.39
  932.5 9.3 all-to-all-start.4
  942.1 2.6 reshape.1973
  944.7 40.2 %gather_fusion.41 = bf16[4096,128]{1,0:T(8,128)(2,1)} fusion(bf16[1,2048,4,128]{3,2,1,0:T(4,128)(2,1)S(1)} %reshape.1973, s32[4096]{0:T(1024)S(1)} %reshape.2369), kind=kCustom, calls=%fused_computation.41 | custom fusion | bytes 2146304 | tf_op jit(solution)/shard_map/vmap()/gather | solution.py:104
  990.9 3.6 fusion
  995.6 104.9 %all-gather.2.cloned.1.call-done = bf16[64,4,4096]{2,1,0:T(4,128)(2,1)} async-done(((bf16[1,4,4096]{2,1,0:T(4,128)(2,1)}), bf16[64,4,4096]{2,1,0:T(4,128)(2,1)}) %all-gather.2.cloned.1.call-update) | async-done | bytes 2097168 | tf_op jit(solution)/shard_map/all_gather | solution.py:177
  1100.5 4.1 fusion.1
  1104.6 12.7 %all-reduce.2 = bf16[64,4,128]{2,0,1:T(8,128)(2,1)S(1)} all-reduce(f32[64,4,128]{2,0,1:T(8,128)S(1)} %fusion.1), channel_id=1, replica_groups=mesh['req'=64,'kvh'=2] {'kvh'}, use_global_device_ids=true, to_apply=%region_170.171 | all-reduce | flops 32768 | bytes 196608 | tf_op jit(solution)/shard_map/psum | solution.py:182
  (922 shorter events, 310.6 us)
Async XLA Ops:
  6.5 1094.0 %copy-start = (bf16[4096,128]{1,0:T(8,128)(2,1)S(1)}, bf16[4096,128]{1,0:T(8,128)(2,1)}, u32[]{:S(2)}) copy-start(bf16[4096,128]{1,0:T(8,128)(2,1)} %param.19) | copy-start | bytes 3145732
  403.2 17.3 %copy-start.207 = (s32[16]{0:T(128)}, s32[16]{0:T(128)S(1)}, u32[]{:S(2)}) copy-start(s32[16]{0:T(128)S(1)} %fusion.401) | copy-start | bytes 196
  409.4 16.7 %copy-start.210 = (s32[16]{0:T(128)}, s32[16]{0:T(128)S(1)}, u32[]{:S(2)}) copy-start(s32[16]{0:T(128)S(1)} %fusion.403) | copy-start | bytes 196
  415.6 13.2 %copy-start.213 = (s32[16]{0:T(128)}, s32[16]{0:T(128)S(1)}, u32[]{:S(2)}) copy-start(s32[16]{0:T(128)S(1)} %fusion.405) | copy-start | bytes 196
  437.1 12.8 %copy-start.57 = (f32[16,1,4,8,256]{4,3,0,2,1:T(8,128)}, f32[16,1,4,8,256]{4,3,0,2,1:T(8,128)S(1)}, u32[]{:S(2)}) copy-start(f32[16,1,4,8,256]{4,3,0,2,1:T(8,128)S(1)} %get-tuple-element.125) | copy-start | bytes 1572868
  502.6 50.7 %all-to-all-start.11 = ((f32[64,1,32]{2,1,0:T(1,128)}), f32[64,1,32]{2,1,0:T(1,128)}, u32[]{:S(2)}, u32[]{:S(2)}) async-start(f32[64,1,32]{2,1,0:T(1,128)} %copy.1020), calls=%async_computation.11 | async-start | bytes 65536 | tf_op jit(solution)/shard_map/all_to_all | solution.py:69
  532.0 21.2 %copy-start.10 = (bf16[1,256,512]{1,2,0:T(8,128)(2,1)}, bf16[1,256,512]{1,2,0:T(8,128)(2,1)S(1)}, u32[]{:S(2)}) copy-start(bf16[1,256,512]{1,2,0:T(8,128)(2,1)S(1)} %copy.1240) | copy-start | bytes 786436
  532.0 30.7 %copy-start.68 = (f32[16,1,4,8,256]{4,3,0,2,1:T(8,128)S(1)}, f32[16,1,4,8,256]{4,3,0,2,1:T(8,128)}, u32[]{:S(2)}) copy-start(f32[16,1,4,8,256]{4,3,0,2,1:T(8,128)} %copy-done.67) | copy-start | bytes 1572868
  532.0 30.7 %copy-start.164 = (f32[16,4,8]{2,0,1:T(8,128)S(1)}, f32[16,4,8]{2,0,1:T(8,128)}, u32[]{:S(2)}) copy-start(f32[16,4,8]{2,0,1:T(8,128)} %copy-done.163) | copy-start | bytes 6148
  544.2 50.1 %copy-start.158 = (f32[16,4,8]{2,0,1:T(8,128)S(1)}, f32[16,4,8]{2,0,1:T(8,128)}, u32[]{:S(2)}) copy-start(f32[16,4,8]{2,0,1:T(8,128)} %copy-done.157) | copy-start | bytes 6148
  553.2 44.5 %copy-start.13 = (bf16[1,256,512]{1,2,0:T(8,128)(2,1)}, bf16[1,256,512]{1,2,0:T(8,128)(2,1)S(1)}, u32[]{:S(2)}) copy-start(bf16[1,256,512]{1,2,0:T(8,128)(2,1)S(1)} %copy.1241) | copy-start | bytes 786436
  553.2 43.2 %copy-start.181 = (f32[16,4,8]{2,0,1:T(8,128)S(1)}, f32[16,4,8]{2,0,1:T(8,128)}, u32[]{:S(2)}) copy-start(f32[16,4,8]{2,0,1:T(8,128)} %get-tuple-element.90) | copy-start | bytes 6148
  553.2 43.8 %copy-start.186 = (f32[16,4,8]{2,0,1:T(8,128)S(1)}, f32[16,4,8]{2,0,1:T(8,128)}, u32[]{:S(2)}) copy-start(f32[16,4,8]{2,0,1:T(8,128)} %get-tuple-element.82) | copy-start | bytes 6148
  553.2 44.4 %copy-start.190 = (f32[16,4,8]{2,0,1:T(8,128)S(1)}, f32[16,4,8]{2,0,1:T(8,128)}, u32[]{:S(2)}) copy-start(f32[16,4,8]{2,0,1:T(8,128)} %get-tuple-element.74) | copy-start | bytes 6148
  553.3 31.8 %all-to-all-start.10 = ((f32[64,1,32]{2,1,0:T(1,128)}), f32[64,1,32]{2,1,0:T(1,128)}, u32[]{:S(2)}, u32[]{:S(2)}) async-start(f32[64,1,32]{2,1,0:T(1,128)} %copy.1009), calls=%async_computation.10 | async-start | bytes 65536 | tf_op jit(solution)/shard_map/all_to_all | solution.py:69
  564.3 33.4 %copy-start.194 = (f32[16,4,8]{2,0,1:T(8,128)S(1)}, f32[16,4,8]{2,0,1:T(8,128)}, u32[]{:S(2)}) copy-start(f32[16,4,8]{2,0,1:T(8,128)} %get-tuple-element.66) | copy-start | bytes 6148
  575.1 47.6 %copy-start.62 = (f32[16,1,4,8,256]{4,3,0,2,1:T(8,128)S(1)}, f32[16,1,4,8,256]{4,3,0,2,1:T(8,128)}, u32[]{:S(2)}) copy-start(f32[16,1,4,8,256]{4,3,0,2,1:T(8,128)} %copy-done.61) | copy-start | bytes 1572868
  575.2 47.6 %copy-start.154 = (f32[16,4,8]{2,0,1:T(8,128)S(1)}, f32[16,4,8]{2,0,1:T(8,128)}, u32[]{:S(2)}) copy-start(f32[16,4,8]{2,0,1:T(8,128)} %copy-done.153) | copy-start | bytes 6148
  585.0 28.0 %all-to-all-start.9 = ((f32[64,1,32]{2,1,0:T(1,128)}), f32[64,1,32]{2,1,0:T(1,128)}, u32[]{:S(2)}, u32[]{:S(2)}) async-start(f32[64,1,32]{2,1,0:T(1,128)} %copy.998), calls=%async_computation.9 | async-start | bytes 65536 | tf_op jit(solution)/shard_map/all_to_all | solution.py:69
  594.3 30.1 %copy-start.176 = (f32[16,4,8]{2,0,1:T(8,128)S(1)}, f32[16,4,8]{2,0,1:T(8,128)}, u32[]{:S(2)}) copy-start(f32[16,4,8]{2,0,1:T(8,128)} %get-tuple-element.89) | copy-start | bytes 6148
  594.3 30.1 %copy-start.179 = (f32[16,4,8]{2,0,1:T(8,128)S(1)}, f32[16,4,8]{2,0,1:T(8,128)}, u32[]{:S(2)}) copy-start(f32[16,4,8]{2,0,1:T(8,128)} %get-tuple-element.81) | copy-start | bytes 6148
  594.3 30.1 %copy-start.184 = (f32[16,4,8]{2,0,1:T(8,128)S(1)}, f32[16,4,8]{2,0,1:T(8,128)}, u32[]{:S(2)}) copy-start(f32[16,4,8]{2,0,1:T(8,128)} %get-tuple-element.73) | copy-start | bytes 6148
  594.4 30.7 %copy-start.188 = (f32[16,4,8]{2,0,1:T(8,128)S(1)}, f32[16,4,8]{2,0,1:T(8,128)}, u32[]{:S(2)}) copy-start(f32[16,4,8]{2,0,1:T(8,128)} %get-tuple-element.65) | copy-start | bytes 6148
  594.4 31.3 %copy-start.193 = (f32[16,4,8]{2,0,1:T(8,128)S(1)}, f32[16,4,8]{2,0,1:T(8,128)}, u32[]{:S(2)}) copy-start(f32[16,4,8]{2,0,1:T(8,128)} %get-tuple-element.57) | copy-start | bytes 6148
  596.4 29.9 %copy-start.196 = (f32[16,4,8]{2,0,1:T(8,128)S(1)}, f32[16,4,8]{2,0,1:T(8,128)}, u32[]{:S(2)}) copy-start(f32[16,4,8]{2,0,1:T(8,128)} %get-tuple-element.49) | copy-start | bytes 6148
  604.0 45.9 %copy-start.146 = (f32[16,4,8]{2,0,1:T(8,128)S(1)}, f32[16,4,8]{2,0,1:T(8,128)}, u32[]{:S(2)}) copy-start(f32[16,4,8]{2,0,1:T(8,128)} %copy-done.145) | copy-start | bytes 6148
  613.0 40.3 %copy-start.16 = (bf16[1,256,512]{1,2,0:T(8,128)(2,1)}, bf16[1,256,512]{1,2,0:T(8,128)(2,1)S(1)}, u32[]{:S(2)}) copy-start(bf16[1,256,512]{1,2,0:T(8,128)(2,1)S(1)} %copy.1242) | copy-start | bytes 786436
  613.0 39.0 %copy-start.173 = (f32[16,4,8]{2,0,1:T(8,128)S(1)}, f32[16,4,8]{2,0,1:T(8,128)}, u32[]{:S(2)}) copy-start(f32[16,4,8]{2,0,1:T(8,128)} %get-tuple-element.88) | copy-start | bytes 6148
  613.0 39.6 %copy-start.175 = (f32[16,4,8]{2,0,1:T(8,128)S(1)}, f32[16,4,8]{2,0,1:T(8,128)}, u32[]{:S(2)}) copy-start(f32[16,4,8]{2,0,1:T(8,128)} %get-tuple-element.80) | copy-start | bytes 6148
  613.1 39.6 %copy-start.178 = (f32[16,4,8]{2,0,1:T(8,128)S(1)}, f32[16,4,8]{2,0,1:T(8,128)}, u32[]{:S(2)}) copy-start(f32[16,4,8]{2,0,1:T(8,128)} %get-tuple-element.72) | copy-start | bytes 6148
  613.1 40.2 %copy-start.183 = (f32[16,4,8]{2,0,1:T(8,128)S(1)}, f32[16,4,8]{2,0,1:T(8,128)}, u32[]{:S(2)}) copy-start(f32[16,4,8]{2,0,1:T(8,128)} %get-tuple-element.64) | copy-start | bytes 6148
  613.1 27.5 %all-to-all-start.8 = ((f32[64,1,32]{2,1,0:T(1,128)}), f32[64,1,32]{2,1,0:T(1,128)}, u32[]{:S(2)}, u32[]{:S(2)}) async-start(f32[64,1,32]{2,1,0:T(1,128)} %copy.987), calls=%async_computation.8 | async-start | bytes 65536 | tf_op jit(solution)/shard_map/all_to_all | solution.py:69
  630.7 47.4 %copy-start.55 = (f32[16,1,4,8,256]{4,3,0,2,1:T(8,128)S(1)}, f32[16,1,4,8,256]{4,3,0,2,1:T(8,128)}, u32[]{:S(2)}) copy-start(f32[16,1,4,8,256]{4,3,0,2,1:T(8,128)} %copy-done.54) | copy-start | bytes 1572868
  630.7 47.4 %copy-start.144 = (f32[16,4,8]{2,0,1:T(8,128)S(1)}, f32[16,4,8]{2,0,1:T(8,128)}, u32[]{:S(2)}) copy-start(f32[16,4,8]{2,0,1:T(8,128)} %copy-done.143) | copy-start | bytes 6148
  640.6 28.1 %all-to-all-start.3 = ((f32[64,1,32]{2,1,0:T(1,128)}), f32[64,1,32]{2,1,0:T(1,128)}, u32[]{:S(2)}, u32[]{:S(2)}) async-start(f32[64,1,32]{2,1,0:T(1,128)} %copy.881), calls=%async_computation.3 | async-start | bytes 65536 | tf_op jit(solution)/shard_map/all_to_all | solution.py:68
  649.9 29.8 %copy-start.170 = (f32[16,4,8]{2,0,1:T(8,128)S(1)}, f32[16,4,8]{2,0,1:T(8,128)}, u32[]{:S(2)}) copy-start(f32[16,4,8]{2,0,1:T(8,128)} %get-tuple-element.87) | copy-start | bytes 6148
  649.9 29.9 %copy-start.172 = (f32[16,4,8]{2,0,1:T(8,128)S(1)}, f32[16,4,8]{2,0,1:T(8,128)}, u32[]{:S(2)}) copy-start(f32[16,4,8]{2,0,1:T(8,128)} %get-tuple-element.79) | copy-start | bytes 6148
  649.9 29.9 %copy-start.174 = (f32[16,4,8]{2,0,1:T(8,128)S(1)}, f32[16,4,8]{2,0,1:T(8,128)}, u32[]{:S(2)}) copy-start(f32[16,4,8]{2,0,1:T(8,128)} %get-tuple-element.71) | copy-start | bytes 6148
  649.9 29.9 %copy-start.177 = (f32[16,4,8]{2,0,1:T(8,128)S(1)}, f32[16,4,8]{2,0,1:T(8,128)}, u32[]{:S(2)}) copy-start(f32[16,4,8]{2,0,1:T(8,128)} %get-tuple-element.63) | copy-start | bytes 6148
  649.9 29.9 %copy-start.182 = (f32[16,4,8]{2,0,1:T(8,128)S(1)}, f32[16,4,8]{2,0,1:T(8,128)}, u32[]{:S(2)}) copy-start(f32[16,4,8]{2,0,1:T(8,128)} %get-tuple-element.55) | copy-start | bytes 6148
  652.0 27.9 %copy-start.187 = (f32[16,4,8]{2,0,1:T(8,128)S(1)}, f32[16,4,8]{2,0,1:T(8,128)}, u32[]{:S(2)}) copy-start(f32[16,4,8]{2,0,1:T(8,128)} %get-tuple-element.47) | copy-start | bytes 6148
  652.0 27.9 %copy-start.191 = (f32[16,4,8]{2,0,1:T(8,128)S(1)}, f32[16,4,8]{2,0,1:T(8,128)}, u32[]{:S(2)}) copy-start(f32[16,4,8]{2,0,1:T(8,128)} %get-tuple-element.39) | copy-start | bytes 6148
  659.1 40.8 %copy-start.138 = (f32[16,4,8]{2,0,1:T(8,128)S(1)}, f32[16,4,8]{2,0,1:T(8,128)}, u32[]{:S(2)}) copy-start(f32[16,4,8]{2,0,1:T(8,128)} %copy-done.137) | copy-start | bytes 6148
  668.6 33.8 %copy-start.19 = (bf16[1,256,512]{1,2,0:T(8,128)(2,1)}, bf16[1,256,512]{1,2,0:T(8,128)(2,1)S(1)}, u32[]{:S(2)}) copy-start(bf16[1,256,512]{1,2,0:T(8,128)(2,1)S(1)} %copy.1243) | copy-start | bytes 786436
  668.6 33.0 %copy-start.168 = (f32[16,4,8]{2,0,1:T(8,128)S(1)}, f32[16,4,8]{2,0,1:T(8,128)}, u32[]{:S(2)}) copy-start(f32[16,4,8]{2,0,1:T(8,128)} %get-tuple-element.86) | copy-start | bytes 6148
  668.6 33.0 %copy-start.169 = (f32[16,4,8]{2,0,1:T(8,128)S(1)}, f32[16,4,8]{2,0,1:T(8,128)}, u32[]{:S(2)}) copy-start(f32[16,4,8]{2,0,1:T(8,128)} %get-tuple-element.78) | copy-start | bytes 6148
  668.7 33.0 %copy-start.171 = (f32[16,4,8]{2,0,1:T(8,128)S(1)}, f32[16,4,8]{2,0,1:T(8,128)}, u32[]{:S(2)}) copy-start(f32[16,4,8]{2,0,1:T(8,128)} %get-tuple-element.70) | copy-start | bytes 6148
  668.7 22.2 %all-to-all-start.2 = ((f32[64,1,32]{2,1,0:T(1,128)}), f32[64,1,32]{2,1,0:T(1,128)}, u32[]{:S(2)}, u32[]{:S(2)}) async-start(f32[64,1,32]{2,1,0:T(1,128)} %copy.854), calls=%async_computation.2 | async-start | bytes 65536 | tf_op jit(solution)/shard_map/all_to_all | solution.py:68
  679.7 23.5 %copy-start.180 = (f32[16,4,8]{2,0,1:T(8,128)S(1)}, f32[16,4,8]{2,0,1:T(8,128)}, u32[]{:S(2)}) copy-start(f32[16,4,8]{2,0,1:T(8,128)} %get-tuple-element.46) | copy-start | bytes 6148
  679.7 23.5 %copy-start.185 = (f32[16,4,8]{2,0,1:T(8,128)S(1)}, f32[16,4,8]{2,0,1:T(8,128)}, u32[]{:S(2)}) copy-start(f32[16,4,8]{2,0,1:T(8,128)} %get-tuple-element.38) | copy-start | bytes 6148
  679.7 23.6 %copy-start.189 = (f32[16,4,8]{2,0,1:T(8,128)S(1)}, f32[16,4,8]{2,0,1:T(8,128)}, u32[]{:S(2)}) copy-start(f32[16,4,8]{2,0,1:T(8,128)} %get-tuple-element.30) | copy-start | bytes 6148
  679.9 42.7 %copy-start.120 = (f32[16,4,8]{2,0,1:T(8,128)S(1)}, f32[16,4,8]{2,0,1:T(8,128)}, u32[]{:S(2)}) copy-start(f32[16,4,8]{2,0,1:T(8,128)} %copy-done.119) | copy-start | bytes 6148
  690.1 34.2 %copy-start.77 = (f32[16,4,8,128]{3,2,0,1:T(8,128)S(1)}, f32[16,4,8,128]{3,2,0,1:T(8,128)}, u32[]{:S(2)}) copy-start(f32[16,4,8,128]{3,2,0,1:T(8,128)} %fusion.85) | copy-start | bytes 786436
  690.9 22.6 %all-to-all-start.1 = ((f32[64,1,32]{2,1,0:T(1,128)}), f32[64,1,32]{2,1,0:T(1,128)S(1)}, u32[]{:S(2)}, u32[]{:S(2)}) async-start(f32[64,1,32]{2,1,0:T(1,128)} %copy.827), calls=%async_computation.1 | async-start | bytes 65536 | tf_op jit(solution)/shard_map/all_to_all | solution.py:68
  699.9 24.4 %copy-start.78 = (f32[16,4,8,128]{3,2,0,1:T(8,128)S(1)}, f32[16,4,8,128]{3,2,0,1:T(8,128)}, u32[]{:S(2)}) copy-start(f32[16,4,8,128]{3,2,0,1:T(8,128)} %fusion.87) | copy-start | bytes 786436
  701.6 22.8 %copy-start.79 = (f32[16,4,8,128]{3,2,0,1:T(8,128)S(1)}, f32[16,4,8,128]{3,2,0,1:T(8,128)}, u32[]{:S(2)}) copy-start(f32[16,4,8,128]{3,2,0,1:T(8,128)} %fusion.89) | copy-start | bytes 786436
  713.5 34.8 %all-to-all-start = ((f32[64,1,32]{2,1,0:T(1,128)}), f32[64,1,32]{2,1,0:T(1,128)S(1)}, u32[]{:S(2)}, u32[]{:S(2)}) async-start(f32[64,1,32]{2,1,0:T(1,128)} %copy.800), calls=%async_computation | async-start | bytes 65536 | tf_op jit(solution)/shard_map/all_to_all | solution.py:68
  748.2 38.9 %all-to-all-start.7 = ((f32[64,1,4096]{2,1,0:T(1,128)}), f32[64,1,4096]{2,1,0:T(1,128)}, u32[]{:S(2)}, u32[]{:S(2)}) async-start(f32[64,1,4096]{2,1,0:T(1,128)} %bitcast.538), calls=%async_computation.7 | async-start | bytes 2097152 | tf_op jit(solution)/shard_map/all_to_all | solution.py:67
  787.2 36.5 %all-to-all-start.6 = ((f32[64,1,4096]{2,1,0:T(1,128)}), f32[64,1,4096]{2,1,0:T(1,128)}, u32[]{:S(2)}, u32[]{:S(2)}) async-start(f32[64,1,4096]{2,1,0:T(1,128)} %bitcast.472), calls=%async_computation.6 | async-start | bytes 2097152 | tf_op jit(solution)/shard_map/all_to_all | solution.py:67
  823.7 108.8 %all-to-all-start.5 = ((f32[64,1,4096]{2,1,0:T(1,128)}), f32[64,1,4096]{2,1,0:T(1,128)}, u32[]{:S(2)}, u32[]{:S(2)}) async-start(f32[64,1,4096]{2,1,0:T(1,128)} %bitcast.406), calls=%async_computation.5 | async-start | bytes 2097152 | tf_op jit(solution)/shard_map/all_to_all | solution.py:67
  932.5 58.5 %all-to-all-start.4 = ((f32[64,1,4096]{2,1,0:T(1,128)}), f32[64,1,4096]{2,1,0:T(1,128)}, u32[]{:S(2)}, u32[]{:S(2)}) async-start(f32[64,1,4096]{2,1,0:T(1,128)} %bitcast.340), calls=%async_computation.4 | async-start | bytes 2097152 | tf_op jit(solution)/shard_map/all_to_all | solution.py:67
  941.8 158.8 %all-gather.2.cloned.1.call-start = ((), (), s32[]{:S(2)}) async-start(), calls=%async_computation.12 | async-start | bytes 2129920 | tf_op jit(solution)/shard_map/all_gather | solution.py:177
  944.6 45.2 %copy-start.206 = (f32[64,1,32]{2,1,0:T(1,128)S(1)}, f32[64,1,32]{2,1,0:T(1,128)}, u32[]{:S(2)}) copy-start(f32[64,1,32]{2,1,0:T(1,128)} %copy-done.205) | copy-start | bytes 24580
  944.7 46.0 %copy-start.243 = (bf16[1,4,512]{2,1,0:T(4,128)(2,1)S(1)}, bf16[1,4,512]{2,1,0:T(4,128)(2,1)}, u32[]{:S(2)}) copy-start(bf16[1,4,512]{2,1,0:T(4,128)(2,1)} %param.12) | copy-start | bytes 12292
  (193 other events, 846.0 us)
Sparse Core Ops, SparseCore 0:
  995.7 104.7 all-gather.1
where the time goes:
time: 1140 us; the launch traced here: 1130 us
  blocking collectives  358 us (31%)
  local copies, waits for them, and re-layouts  245 us (21%)
  other arithmetic  205 us (18%)
  starting transfers between devices  109 us (10%)
  waiting for transfers between devices  105 us (9%)
  matrix products  83.1 us (7%)
  between operations  19.2 us (2%)
    all_gather x4, blocking collectives, local(): lax.all_gather(queries[:, step_index:step_index + 1], 'req', axis=0, tile...  325 us
    all_gather x1, waiting for transfers between devices, local(): piece_rows = lax.all_gather(attention, 'req', axis=0, tiled=True)  105 us
    scatter-add x32, other arithmetic, prefix_partials(): out_all.at[slot_rows].add(jnp.where(is_valid[..., None], part_out, 0.0))  78.6 us
    gather x4, local copies, waits for them, and re-layouts, local(): key_table[pick_list.T, head_index_list]  66.8 us
    dot_general x32, matrix products, prefix_partials(): jnp.einsum('cskgl,lkd->cskgd', weights, stretch_values, preferred_element...  44.8 us
    gather x1, local copies, waits for them, and re-layouts, local(): value_table[pick_list.T, head_index_list]  40.2 us
    scatter-add x32, other arithmetic, prefix_partials(): total_all = total_all.at[slot_rows].add(jnp.where(is_valid, row_total, 0.0))  39.9 us
    scatter-add x32, other arithmetic, prefix_partials(): peak_all = peak_all.at[slot_rows].add(jnp.where(is_valid, row_peak, 0.0))  39.9 us
  transfers between devices with their start and end apart: 13, of which 1 were waited for; matrix products, arithmetic and copies ran while one was open for 33% of the time, Pallas kernels for 0%

commit v1 on v0

--- a/solution.py
+++ b/solution.py
@@ -136,7 +136,15 @@
     partial_sets = []
     for step_index in range(step_count):
         query_all, member_all = (
-            lax.all_gather(queries[:, step_index : step_index + 1], "req", axis=0, tiled=True),
+            jnp.concatenate(
+                lax.all_to_all(
+                    jnp.stack([queries[:, step_index : step_index + 1]] * lax.axis_size("req")),
+                    "req",
+                    0,
+                    0,
+                ),
+                axis=0,
+            ),
             lax.all_gather(membership, "req", axis=0, tiled=True),
         )
         partial_sets.append(

time: 1140 us -> 892 us (0.78)
  blocking collectives: 358 us -> 32.9 us
  matrix products: 83.1 us -> 43.5 us
  other arithmetic: 205 us -> 240 us
  local copies, waits for them, and re-layouts: 245 us -> 277 us
  starting transfers between devices: 109 us -> 138 us
  waiting for transfers between devices: 105 us -> 126 us
    all_gather x4 -> x0, blocking collectives: 325 us -> none  [local(): lax.all_gather(queries[:, step_index:step_index + 1], 'req', axis=0, tile...]
    all_to_all x0 -> x4, starting transfers between devices: none -> 24.8 us  [local(): lax.all_to_all(jnp.stack([queries[:, step_index:step_index + 1]] * lax.ax...]
    unnamed x511 -> x535, local copies, waits for them, and re-layouts: 22.4 us -> 47.2 us
    gather x4, local copies, waits for them, and re-layouts: 66.8 us -> 42.5 us  [local(): key_table[pick_list.T, head_index_list]]
    all_to_all x0 -> x4, waiting for transfers between devices: none -> 21.3 us  [local(): lax.all_to_all(jnp.stack([queries[:, step_index:step_index + 1]] * lax.ax...]
    dot_general x32, matrix products: 32.9 us -> 11.6 us  [prefix_partials(): jnp.einsum('cskgd,lkd->cskgl', chosen_index, stretch_keys, preferred_elem...]
    dot_general x32, matrix products: 44.8 us -> 25.3 us  [prefix_partials(): jnp.einsum('cskgl,lkd->cskgd', weights, stretch_values, preferred_element...]
    select_n x32, local copies, waits for them, and re-layouts: 10.9 us -> 28.4 us  [prefix_partials(): peak_all = peak_all.at[slot_rows].add(jnp.where(is_valid, row_peak, 0.0))]
  transfers between devices with their start and end apart: 13 -> 17, of which waited for: 1 -> 3; matrix products, arithmetic and copies ran while one was open for 33% -> 51% of each run, Pallas kernels for 0% -> 0%
where the time goes in v1:
time: 892 us; the launch traced here: 876 us
  local copies, waits for them, and re-layouts  277 us (31%)
  other arithmetic  240 us (27%)
  starting transfers between devices  138 us (15%)
  waiting for transfers between devices  126 us (14%)
  matrix products  43.5 us (5%)
  blocking collectives  32.9 us (4%)
  between operations  19.2 us (2%)
    all_gather x1, waiting for transfers between devices, local(): piece_rows = lax.all_gather(attention, 'req', axis=0, tiled=True)  105 us
    scatter-add x32, other arithmetic, prefix_partials(): out_all.at[slot_rows].add(jnp.where(is_valid[..., None], part_out, 0.0))  79.1 us
    scatter-add x32, other arithmetic, prefix_partials(): total_all = total_all.at[slot_rows].add(jnp.where(is_valid, row_total, 0.0))  49.3 us
    unnamed x535, local copies, waits for them, and re-layouts  47.2 us
    scatter-add x32, other arithmetic, prefix_partials(): peak_all = peak_all.at[slot_rows].add(jnp.where(is_valid, row_peak, 0.0))  44.9 us
    gather x4, local copies, waits for them, and re-layouts, local(): key_table[pick_list.T, head_index_list]  42.5 us
    gather x32, local copies, waits for them, and re-layouts, prefix_partials(): chosen_index = grouped_query_heads[slot_rows]  41 us
    gather x1, local copies, waits for them, and re-layouts, local(): value_table[pick_list.T, head_index_list]  40.1 us
  transfers between devices with their start and end apart: 17, of which 3 were waited for; matrix products, arithmetic and copies ran while one was open for 51% of the time, Pallas kernels for 0%

profile of v1, /device:TPU:0, one launch (start us, length us, event | category | flops | bytes accessed | tf_op | source)
XLA Modules:
  0.0 876.1 jit_solution(17478132950932574918)
XLA Ops:
  9.2 4.6 reduce.83
  16.1 9.7 %all-to-all-start = ((bf16[64,2,2048]{2,1,0:T(2,128)(2,1)}), bf16[64,2,2048]{2,1,0:T(2,128)(2,1)}, u32[]{:S(2)}, u32[]{:S(2)}) async-start(bf16[64,2,2048]{2,1,0:T(2,128)(2,1)} %reshape.3592), calls=%async_computation | async-start | bytes 1048576 | tf_op jit(solution)/shard_map/all_to_all | solution.py:140
  27.7 20.2 %all-reduce = s32[64]{0:T(128)S(1)} all-reduce(s32[64]{0:T(128)S(1)} %bitcast_dynamic-update-slice_fusion), channel_id=1, replica_groups=mesh['req'=64,'kvh'=2] {'req'}, use_global_device_ids=true, to_apply=%add | all-reduce | flops 64 | bytes 512 | tf_op jit(solution)/shard_map/squeeze | solution.py:24
  58.2 3.8 reduce.84
  64.2 3.8 reduce.85
  70.2 4.0 reduce.86
  97.3 2.6 reshape.1929
  102.3 2.8 fusion.408
  117.8 40.2 %gather_fusion.40 = bf16[4096,128]{1,0:T(8,128)(2,1)} fusion(bf16[1,2048,4,128]{3,2,1,0:T(4,128)(2,1)S(1)} %reshape.1929, s32[4096]{0:T(1024)S(1)} %reshape.2365), kind=kCustom, calls=%fused_computation.40 | custom fusion | bytes 2146304 | tf_op jit(solution)/shard_map/vmap()/gather | solution.py:100
  159.3 4.6 all-to-all-start.2
  164.5 11.3 %all-to-all-done.2 = bf16[64,2,2048]{2,1,0:T(2,128)(2,1)S(1)} async-done(((bf16[64,2,2048]{2,1,0:T(2,128)(2,1)}), bf16[64,2,2048]{2,1,0:T(2,128)(2,1)S(1)}, u32[]{:S(2)}, u32[]{:S(2)}) %all-to-all-start.2) | async-done | bytes 524320 | tf_op jit(solution)/shard_map/all_to_all | solution.py:140
  175.8 4.6 all-to-all-start.4
  182.3 10.0 %all-to-all-done.4 = bf16[64,2,2048]{2,1,0:T(2,128)(2,1)S(1)} async-done(((bf16[64,2,2048]{2,1,0:T(2,128)(2,1)}), bf16[64,2,2048]{2,1,0:T(2,128)(2,1)S(1)}, u32[]{:S(2)}, u32[]{:S(2)}) %all-to-all-start.4) | async-done | bytes 524320 | tf_op jit(solution)/shard_map/all_to_all | solution.py:140
  192.3 5.9 all-to-all-start.6
  201.1 3.6 reshape.3593
  204.8 3.1 reduce.72
  208.6 3.1 reduce.74
  216.7 3.6 reshape.3589
  220.3 3.9 reduce.76
  227.8 4.6 reshape.3587
  232.4 5.1 reduce.78
  318.7 9.7 %all-to-all-start.15 = ((f32[64,1,32]{2,1,0:T(1,128)}), f32[64,1,32]{2,1,0:T(1,128)}, u32[]{:S(2)}, u32[]{:S(2)}) async-start(f32[64,1,32]{2,1,0:T(1,128)} %copy.1020), calls=%async_computation.15 | async-start | bytes 65536 | tf_op jit(solution)/shard_map/all_to_all | solution.py:69
  349.5 9.3 %all-to-all-start.14 = ((f32[64,1,32]{2,1,0:T(1,128)}), f32[64,1,32]{2,1,0:T(1,128)}, u32[]{:S(2)}, u32[]{:S(2)}) async-start(f32[64,1,32]{2,1,0:T(1,128)} %copy.1009), calls=%async_computation.14 | async-start | bytes 65536 | tf_op jit(solution)/shard_map/all_to_all | solution.py:69
  383.4 9.3 %all-to-all-start.13 = ((f32[64,1,32]{2,1,0:T(1,128)}), f32[64,1,32]{2,1,0:T(1,128)}, u32[]{:S(2)}, u32[]{:S(2)}) async-start(f32[64,1,32]{2,1,0:T(1,128)} %copy.998), calls=%async_computation.13 | async-start | bytes 65536 | tf_op jit(solution)/shard_map/all_to_all | solution.py:69
  421.1 9.3 %all-to-all-start.12 = ((f32[64,1,32]{2,1,0:T(1,128)}), f32[64,1,32]{2,1,0:T(1,128)}, u32[]{:S(2)}, u32[]{:S(2)}) async-start(f32[64,1,32]{2,1,0:T(1,128)} %copy.987), calls=%async_computation.12 | async-start | bytes 65536 | tf_op jit(solution)/shard_map/all_to_all | solution.py:69
  458.9 9.3 %all-to-all-start.7 = ((f32[64,1,32]{2,1,0:T(1,128)}), f32[64,1,32]{2,1,0:T(1,128)}, u32[]{:S(2)}, u32[]{:S(2)}) async-start(f32[64,1,32]{2,1,0:T(1,128)} %copy.881), calls=%async_computation.7 | async-start | bytes 65536 | tf_op jit(solution)/shard_map/all_to_all | solution.py:68
  496.6 9.3 %all-to-all-start.5 = ((f32[64,1,32]{2,1,0:T(1,128)}), f32[64,1,32]{2,1,0:T(1,128)}, u32[]{:S(2)}, u32[]{:S(2)}) async-start(f32[64,1,32]{2,1,0:T(1,128)} %copy.854), calls=%async_computation.5 | async-start | bytes 65536 | tf_op jit(solution)/shard_map/all_to_all | solution.py:68
  524.1 9.5 %all-to-all-start.3 = ((f32[64,1,32]{2,1,0:T(1,128)}), f32[64,1,32]{2,1,0:T(1,128)}, u32[]{:S(2)}, u32[]{:S(2)}) async-start(f32[64,1,32]{2,1,0:T(1,128)} %copy.827), calls=%async_computation.3 | async-start | bytes 65536 | tf_op jit(solution)/shard_map/all_to_all | solution.py:68
  545.7 9.0 %all-to-all-start.1 = ((f32[64,1,32]{2,1,0:T(1,128)}), f32[64,1,32]{2,1,0:T(1,128)S(1)}, u32[]{:S(2)}, u32[]{:S(2)}) async-start(f32[64,1,32]{2,1,0:T(1,128)} %copy.800), calls=%async_computation.1 | async-start | bytes 65536 | tf_op jit(solution)/shard_map/all_to_all | solution.py:68
  560.6 2.7 scatter_fusion.56
  563.3 2.7 scatter_fusion.57
  565.9 2.4 scatter_fusion.58
  573.2 2.4 scatter_fusion.61
  575.7 2.4 scatter_fusion.62
  578.1 2.6 scatter_fusion.63
  580.8 9.5 %all-to-all-start.11 = ((f32[64,1,4096]{2,1,0:T(1,128)}), f32[64,1,4096]{2,1,0:T(1,128)}, u32[]{:S(2)}, u32[]{:S(2)}) async-start(f32[64,1,4096]{2,1,0:T(1,128)} %bitcast.538), calls=%async_computation.11 | async-start | bytes 2097152 | tf_op jit(solution)/shard_map/all_to_all | solution.py:67
  595.1 2.4 scatter_fusion.48
  597.6 2.4 scatter_fusion.49
  600.0 2.4 scatter_fusion.50
  602.4 2.4 scatter_fusion.51
  604.8 2.4 scatter_fusion.52
  607.3 2.4 scatter_fusion.53
  612.1 2.6 scatter_fusion.55
  614.8 9.6 %all-to-all-start.10 = ((f32[64,1,4096]{2,1,0:T(1,128)}), f32[64,1,4096]{2,1,0:T(1,128)}, u32[]{:S(2)}, u32[]{:S(2)}) async-start(f32[64,1,4096]{2,1,0:T(1,128)} %bitcast.472), calls=%async_computation.10 | async-start | bytes 2097152 | tf_op jit(solution)/shard_map/all_to_all | solution.py:67
  631.4 2.4 scatter_fusion.41
  633.8 2.4 scatter_fusion.42
  638.7 2.4 scatter_fusion.44
  646.0 2.7 scatter_fusion.47
  648.7 9.7 %all-to-all-start.9 = ((f32[64,1,4096]{2,1,0:T(1,128)}), f32[64,1,4096]{2,1,0:T(1,128)}, u32[]{:S(2)}, u32[]{:S(2)}) async-start(f32[64,1,4096]{2,1,0:T(1,128)} %bitcast.406), calls=%async_computation.9 | async-start | bytes 2097152 | tf_op jit(solution)/shard_map/all_to_all | solution.py:67
  662.9 2.4 scatter_fusion.32
  665.3 2.4 scatter_fusion.33
  667.7 2.4 scatter_fusion.34
  670.1 2.4 scatter_fusion.35
  672.6 2.4 scatter_fusion.36
  675.0 2.4 scatter_fusion.37
  677.4 2.4 scatter_fusion.38
  679.9 2.6 scatter_fusion.39
  682.5 9.4 %all-to-all-start.8 = ((f32[64,1,4096]{2,1,0:T(1,128)}), f32[64,1,4096]{2,1,0:T(1,128)}, u32[]{:S(2)}, u32[]{:S(2)}) async-start(f32[64,1,4096]{2,1,0:T(1,128)} %bitcast.340), calls=%async_computation.8 | async-start | bytes 2097152 | tf_op jit(solution)/shard_map/all_to_all | solution.py:67
  692.1 2.8 reshape.1969
  695.0 40.1 %gather_fusion.41 = bf16[4096,128]{1,0:T(8,128)(2,1)} fusion(bf16[1,2048,4,128]{3,2,1,0:T(4,128)(2,1)S(1)} %reshape.1969, s32[4096]{0:T(1024)S(1)} %copy-done.2), kind=kCustom, calls=%fused_computation.41 | custom fusion | bytes 2146304 | tf_op jit(solution)/shard_map/vmap()/gather | solution.py:104
  742.0 3.6 fusion
  746.6 104.9 %all-gather.2.cloned.1.call-done = bf16[64,4,4096]{2,1,0:T(4,128)(2,1)} async-done(((bf16[1,4,4096]{2,1,0:T(4,128)(2,1)}), bf16[64,4,4096]{2,1,0:T(4,128)(2,1)}) %all-gather.2.cloned.1.call-update) | async-done | bytes 2097168 | tf_op jit(solution)/shard_map/all_gather | solution.py:185
  851.6 4.1 fusion.1
  855.6 12.7 %all-reduce.2 = bf16[64,4,128]{2,0,1:T(8,128)(2,1)S(1)} all-reduce(f32[64,4,128]{2,0,1:T(8,128)S(1)} %fusion.1), channel_id=1, replica_groups=mesh['req'=64,'kvh'=2] {'kvh'}, use_global_device_ids=true, to_apply=%region_170.171 | all-reduce | flops 32768 | bytes 196608 | tf_op jit(solution)/shard_map/psum | solution.py:190
  (959 shorter events, 358.5 us)
Async XLA Ops:
  6.5 845.0 %copy-start = (bf16[4096,128]{1,0:T(8,128)(2,1)S(1)}, bf16[4096,128]{1,0:T(8,128)(2,1)}, u32[]{:S(2)}) copy-start(bf16[4096,128]{1,0:T(8,128)(2,1)} %param.19) | copy-start | bytes 3145732
  8.6 17.8 %copy-start.251 = (u32[128]{0:T(128)S(1)}, u32[128]{0:T(128)}, u32[]{:S(2)}) copy-start(u32[128]{0:T(128)} %constant.79) | copy-start | bytes 1540
  13.7 39.2 %copy-start.91 = (bf16[8,256,512]{2,1,0:T(8,128)(2,1)S(1)}, bf16[8,256,512]{2,1,0:T(8,128)(2,1)}, u32[]{:S(2)}) copy-start(bf16[8,256,512]{2,1,0:T(8,128)(2,1)} %param.13) | copy-start | bytes 6291460
  16.1 143.2 %all-to-all-start = ((bf16[64,2,2048]{2,1,0:T(2,128)(2,1)}), bf16[64,2,2048]{2,1,0:T(2,128)(2,1)}, u32[]{:S(2)}, u32[]{:S(2)}) async-start(bf16[64,2,2048]{2,1,0:T(2,128)(2,1)} %reshape.3592), calls=%async_computation | async-start | bytes 1048576 | tf_op jit(solution)/shard_map/all_to_all | solution.py:140
  75.4 12.3 %copy-start.95 = (bf16[1,256,512]{2,1,0:T(8,128)(2,1)S(1)}, bf16[1,256,512]{2,1,0:T(8,128)(2,1)}, u32[]{:S(2)}) copy-start(bf16[1,256,512]{2,1,0:T(8,128)(2,1)} %get-tuple-element.25) | copy-start | bytes 786436
  76.8 14.2 %copy-start.94 = (bf16[1,256,512]{2,1,0:T(8,128)(2,1)S(1)}, bf16[1,256,512]{2,1,0:T(8,128)(2,1)}, u32[]{:S(2)}) copy-start(bf16[1,256,512]{2,1,0:T(8,128)(2,1)} %get-tuple-element.24) | copy-start | bytes 786436
  81.0 13.2 %copy-start.93 = (bf16[1,256,512]{2,1,0:T(8,128)(2,1)S(1)}, bf16[1,256,512]{2,1,0:T(8,128)(2,1)}, u32[]{:S(2)}) copy-start(bf16[1,256,512]{2,1,0:T(8,128)(2,1)} %get-tuple-element.23) | copy-start | bytes 786436
  84.4 12.0 %copy-start.92 = (bf16[1,256,512]{2,1,0:T(8,128)(2,1)S(1)}, bf16[1,256,512]{2,1,0:T(8,128)(2,1)}, u32[]{:S(2)}) copy-start(bf16[1,256,512]{2,1,0:T(8,128)(2,1)} %get-tuple-element.22) | copy-start | bytes 786436
  102.3 15.5 %copy-start.1 = (s32[4096]{0:T(1024)}, s32[4096]{0:T(1024)S(1)}, u32[]{:S(2)}) copy-start(s32[4096]{0:T(1024)S(1)} %reshape.2365) | copy-start | bytes 49156
  117.8 436.9 %copy-start.4 = (bf16[1,256,512]{1,2,0:T(8,128)(2,1)}, bf16[1,256,512]{1,2,0:T(8,128)(2,1)S(1)}, u32[]{:S(2)}) copy-start(bf16[1,256,512]{1,2,0:T(8,128)(2,1)S(1)} %copy.1243) | copy-start | bytes 786436
  157.9 40.3 %copy-start.107 = (bf16[4096,128]{1,0:T(8,128)(2,1)S(1)}, bf16[4096,128]{1,0:T(8,128)(2,1)}, u32[]{:S(2)}) copy-start(bf16[4096,128]{1,0:T(8,128)(2,1)} %gather_fusion.40) | copy-start | bytes 3145732
  157.9 40.3 %copy-start.215 = (bf16[1,4,4096]{2,1,0:T(4,128)(2,1)S(1)}, bf16[1,4,4096]{2,1,0:T(4,128)(2,1)}, u32[]{:S(2)}) copy-start(bf16[1,4,4096]{2,1,0:T(4,128)(2,1)} %param.10) | copy-start | bytes 98308
  159.3 39.5 %copy-start.216 = (s32[16]{0:T(128)}, s32[16]{0:T(128)S(1)}, u32[]{:S(2)}) copy-start(s32[16]{0:T(128)S(1)} %fusion.401) | copy-start | bytes 196
  159.3 16.5 %all-to-all-start.2 = ((bf16[64,2,2048]{2,1,0:T(2,128)(2,1)}), bf16[64,2,2048]{2,1,0:T(2,128)(2,1)S(1)}, u32[]{:S(2)}, u32[]{:S(2)}) async-start(bf16[64,2,2048]{2,1,0:T(2,128)(2,1)} %reshape.3590), calls=%async_computation.2 | async-start | bytes 1048576 | tf_op jit(solution)/shard_map/all_to_all | solution.py:140
  164.5 35.1 %copy-start.218 = (s32[16]{0:T(128)}, s32[16]{0:T(128)S(1)}, u32[]{:S(2)}) copy-start(s32[16]{0:T(128)S(1)} %fusion.405) | copy-start | bytes 196
  164.5 35.1 %copy-start.249 = (bf16[1,4,512]{2,1,0:T(4,128)(2,1)S(1)}, bf16[1,4,512]{2,1,0:T(4,128)(2,1)}, u32[]{:S(2)}) copy-start(bf16[1,4,512]{2,1,0:T(4,128)(2,1)} %param.11) | copy-start | bytes 12292
  175.8 16.5 %all-to-all-start.4 = ((bf16[64,2,2048]{2,1,0:T(2,128)(2,1)}), bf16[64,2,2048]{2,1,0:T(2,128)(2,1)S(1)}, u32[]{:S(2)}, u32[]{:S(2)}) async-start(bf16[64,2,2048]{2,1,0:T(2,128)(2,1)} %reshape.3588), calls=%async_computation.4 | async-start | bytes 1048576 | tf_op jit(solution)/shard_map/all_to_all | solution.py:140
  181.7 23.0 %copy-start.222 = (s32[16]{0:T(128)}, s32[16]{0:T(128)S(1)}, u32[]{:S(2)}) copy-start(s32[16]{0:T(128)S(1)} %fusion.407) | copy-start | bytes 196
  192.3 35.5 %all-to-all-start.6 = ((bf16[64,2,2048]{2,1,0:T(2,128)(2,1)}), bf16[64,2,2048]{2,1,0:T(2,128)(2,1)}, u32[]{:S(2)}, u32[]{:S(2)}) async-start(bf16[64,2,2048]{2,1,0:T(2,128)(2,1)} %reshape.3586), calls=%async_computation.6 | async-start | bytes 1048576 | tf_op jit(solution)/shard_map/all_to_all | solution.py:140
  250.8 21.7 %copy-start.40 = (bf16[1,256,512]{1,2,0:T(8,128)(2,1)S(1)}, bf16[1,256,512]{1,2,0:T(8,128)(2,1)}, u32[]{:S(2)}) copy-start(bf16[1,256,512]{1,2,0:T(8,128)(2,1)} %copy.1228) | copy-start | bytes 786436
  304.0 11.3 %copy-start.178 = (f32[16,4,8]{2,0,1:T(8,128)}, f32[16,4,8]{2,0,1:T(8,128)S(1)}, u32[]{:S(2)}) copy-start(f32[16,4,8]{2,0,1:T(8,128)S(1)} %get-tuple-element.174) | copy-start | bytes 6148
  304.0 24.4 %copy-start.27 = (bf16[1,256,512]{1,2,0:T(8,128)(2,1)S(1)}, bf16[1,256,512]{1,2,0:T(8,128)(2,1)}, u32[]{:S(2)}) copy-start(bf16[1,256,512]{1,2,0:T(8,128)(2,1)} %copy.1237) | copy-start | bytes 786436
  316.6 42.2 %copy-start.24 = (bf16[1,256,512]{1,2,0:T(8,128)(2,1)S(1)}, bf16[1,256,512]{1,2,0:T(8,128)(2,1)}, u32[]{:S(2)}) copy-start(bf16[1,256,512]{1,2,0:T(8,128)(2,1)} %copy.1238) | copy-start | bytes 786436
  317.3 15.3 %copy-start.200 = (f32[16,4,8]{2,0,1:T(8,128)S(1)}, f32[16,4,8]{2,0,1:T(8,128)}, u32[]{:S(2)}) copy-start(f32[16,4,8]{2,0,1:T(8,128)} %get-tuple-element.92) | copy-start | bytes 6148
  317.3 41.5 %copy-start.187 = (f32[16,4,8]{2,0,1:T(8,128)S(1)}, f32[16,4,8]{2,0,1:T(8,128)}, u32[]{:S(2)}) copy-start(f32[16,4,8]{2,0,1:T(8,128)} %copy-done.186) | copy-start | bytes 6148
  318.7 30.8 %all-to-all-start.15 = ((f32[64,1,32]{2,1,0:T(1,128)}), f32[64,1,32]{2,1,0:T(1,128)}, u32[]{:S(2)}, u32[]{:S(2)}) async-start(f32[64,1,32]{2,1,0:T(1,128)} %copy.1020), calls=%async_computation.15 | async-start | bytes 65536 | tf_op jit(solution)/shard_map/all_to_all | solution.py:69
  330.5 30.3 %copy-start.197 = (f32[16,4,8]{2,0,1:T(8,128)S(1)}, f32[16,4,8]{2,0,1:T(8,128)}, u32[]{:S(2)}) copy-start(f32[16,4,8]{2,0,1:T(8,128)} %get-tuple-element.91) | copy-start | bytes 6148
  330.5 30.9 %copy-start.199 = (f32[16,4,8]{2,0,1:T(8,128)S(1)}, f32[16,4,8]{2,0,1:T(8,128)}, u32[]{:S(2)}) copy-start(f32[16,4,8]{2,0,1:T(8,128)} %get-tuple-element.83) | copy-start | bytes 6148
  332.6 29.4 %copy-start.201 = (f32[16,4,8]{2,0,1:T(8,128)S(1)}, f32[16,4,8]{2,0,1:T(8,128)}, u32[]{:S(2)}) copy-start(f32[16,4,8]{2,0,1:T(8,128)} %get-tuple-element.75) | copy-start | bytes 6148
  332.6 30.1 %copy-start.204 = (f32[16,4,8]{2,0,1:T(8,128)S(1)}, f32[16,4,8]{2,0,1:T(8,128)}, u32[]{:S(2)}) copy-start(f32[16,4,8]{2,0,1:T(8,128)} %get-tuple-element.67) | copy-start | bytes 6148
  332.6 30.7 %copy-start.207 = (f32[16,4,8]{2,0,1:T(8,128)S(1)}, f32[16,4,8]{2,0,1:T(8,128)}, u32[]{:S(2)}) copy-start(f32[16,4,8]{2,0,1:T(8,128)} %get-tuple-element.59) | copy-start | bytes 6148
  349.5 34.0 %all-to-all-start.14 = ((f32[64,1,32]{2,1,0:T(1,128)}), f32[64,1,32]{2,1,0:T(1,128)}, u32[]{:S(2)}, u32[]{:S(2)}) async-start(f32[64,1,32]{2,1,0:T(1,128)} %copy.1009), calls=%async_computation.14 | async-start | bytes 65536 | tf_op jit(solution)/shard_map/all_to_all | solution.py:69
  363.9 66.5 %copy-start.20 = (bf16[1,256,512]{1,2,0:T(8,128)(2,1)S(1)}, bf16[1,256,512]{1,2,0:T(8,128)(2,1)}, u32[]{:S(2)}) copy-start(bf16[1,256,512]{1,2,0:T(8,128)(2,1)} %copy.1239) | copy-start | bytes 786436
  383.4 37.7 %all-to-all-start.13 = ((f32[64,1,32]{2,1,0:T(1,128)}), f32[64,1,32]{2,1,0:T(1,128)}, u32[]{:S(2)}, u32[]{:S(2)}) async-start(f32[64,1,32]{2,1,0:T(1,128)} %copy.998), calls=%async_computation.13 | async-start | bytes 65536 | tf_op jit(solution)/shard_map/all_to_all | solution.py:69
  401.6 66.6 %copy-start.16 = (bf16[1,256,512]{1,2,0:T(8,128)(2,1)S(1)}, bf16[1,256,512]{1,2,0:T(8,128)(2,1)}, u32[]{:S(2)}) copy-start(bf16[1,256,512]{1,2,0:T(8,128)(2,1)} %copy.1240) | copy-start | bytes 786436
  421.1 37.7 %all-to-all-start.12 = ((f32[64,1,32]{2,1,0:T(1,128)}), f32[64,1,32]{2,1,0:T(1,128)}, u32[]{:S(2)}, u32[]{:S(2)}) async-start(f32[64,1,32]{2,1,0:T(1,128)} %copy.987), calls=%async_computation.12 | async-start | bytes 65536 | tf_op jit(solution)/shard_map/all_to_all | solution.py:69
  439.3 66.6 %copy-start.12 = (bf16[1,256,512]{1,2,0:T(8,128)(2,1)S(1)}, bf16[1,256,512]{1,2,0:T(8,128)(2,1)}, u32[]{:S(2)}) copy-start(bf16[1,256,512]{1,2,0:T(8,128)(2,1)} %copy.1241) | copy-start | bytes 786436
  458.9 37.8 %all-to-all-start.7 = ((f32[64,1,32]{2,1,0:T(1,128)}), f32[64,1,32]{2,1,0:T(1,128)}, u32[]{:S(2)}, u32[]{:S(2)}) async-start(f32[64,1,32]{2,1,0:T(1,128)} %copy.881), calls=%async_computation.7 | async-start | bytes 65536 | tf_op jit(solution)/shard_map/all_to_all | solution.py:68
  477.1 56.5 %copy-start.8 = (bf16[1,256,512]{1,2,0:T(8,128)(2,1)S(1)}, bf16[1,256,512]{1,2,0:T(8,128)(2,1)}, u32[]{:S(2)}) copy-start(bf16[1,256,512]{1,2,0:T(8,128)(2,1)} %copy.1242) | copy-start | bytes 786436
  495.2 38.4 %copy-start.181 = (f32[16,4,8]{2,0,1:T(8,128)S(1)}, f32[16,4,8]{2,0,1:T(8,128)}, u32[]{:S(2)}) copy-start(f32[16,4,8]{2,0,1:T(8,128)} %copy-done.180) | copy-start | bytes 6148
  495.2 40.1 %copy-start.190 = (f32[16,4,8]{2,0,1:T(8,128)S(1)}, f32[16,4,8]{2,0,1:T(8,128)}, u32[]{:S(2)}) copy-start(f32[16,4,8]{2,0,1:T(8,128)} %get-tuple-element.86) | copy-start | bytes 6148
  495.2 40.1 %copy-start.191 = (f32[16,4,8]{2,0,1:T(8,128)S(1)}, f32[16,4,8]{2,0,1:T(8,128)}, u32[]{:S(2)}) copy-start(f32[16,4,8]{2,0,1:T(8,128)} %get-tuple-element.78) | copy-start | bytes 6148
  495.2 40.1 %copy-start.192 = (f32[16,4,8]{2,0,1:T(8,128)S(1)}, f32[16,4,8]{2,0,1:T(8,128)}, u32[]{:S(2)}) copy-start(f32[16,4,8]{2,0,1:T(8,128)} %get-tuple-element.70) | copy-start | bytes 6148
  496.6 27.4 %all-to-all-start.5 = ((f32[64,1,32]{2,1,0:T(1,128)}), f32[64,1,32]{2,1,0:T(1,128)}, u32[]{:S(2)}, u32[]{:S(2)}) async-start(f32[64,1,32]{2,1,0:T(1,128)} %copy.854), calls=%async_computation.5 | async-start | bytes 65536 | tf_op jit(solution)/shard_map/all_to_all | solution.py:68
  507.7 27.7 %copy-start.193 = (f32[16,4,8]{2,0,1:T(8,128)S(1)}, f32[16,4,8]{2,0,1:T(8,128)}, u32[]{:S(2)}) copy-start(f32[16,4,8]{2,0,1:T(8,128)} %get-tuple-element.62) | copy-start | bytes 6148
  507.7 27.7 %copy-start.194 = (f32[16,4,8]{2,0,1:T(8,128)S(1)}, f32[16,4,8]{2,0,1:T(8,128)}, u32[]{:S(2)}) copy-start(f32[16,4,8]{2,0,1:T(8,128)} %get-tuple-element.54) | copy-start | bytes 6148
  507.7 27.8 %copy-start.195 = (f32[16,4,8]{2,0,1:T(8,128)S(1)}, f32[16,4,8]{2,0,1:T(8,128)}, u32[]{:S(2)}) copy-start(f32[16,4,8]{2,0,1:T(8,128)} %get-tuple-element.46) | copy-start | bytes 6148
  507.7 27.8 %copy-start.196 = (f32[16,4,8]{2,0,1:T(8,128)S(1)}, f32[16,4,8]{2,0,1:T(8,128)}, u32[]{:S(2)}) copy-start(f32[16,4,8]{2,0,1:T(8,128)} %get-tuple-element.38) | copy-start | bytes 6148
  507.7 27.8 %copy-start.198 = (f32[16,4,8]{2,0,1:T(8,128)S(1)}, f32[16,4,8]{2,0,1:T(8,128)}, u32[]{:S(2)}) copy-start(f32[16,4,8]{2,0,1:T(8,128)} %get-tuple-element.30) | copy-start | bytes 6148
  511.6 43.1 %copy-start.179 = (f32[16,4,8]{2,0,1:T(8,128)S(1)}, f32[16,4,8]{2,0,1:T(8,128)}, u32[]{:S(2)}) copy-start(f32[16,4,8]{2,0,1:T(8,128)} %copy-done.178) | copy-start | bytes 6148
  523.3 32.4 %copy-start.99 = (f32[16,4,8,128]{3,2,0,1:T(8,128)S(1)}, f32[16,4,8,128]{3,2,0,1:T(8,128)}, u32[]{:S(2)}) copy-start(f32[16,4,8,128]{3,2,0,1:T(8,128)} %fusion.85) | copy-start | bytes 786436
  524.1 21.6 %all-to-all-start.3 = ((f32[64,1,32]{2,1,0:T(1,128)}), f32[64,1,32]{2,1,0:T(1,128)}, u32[]{:S(2)}, u32[]{:S(2)}) async-start(f32[64,1,32]{2,1,0:T(1,128)} %copy.827), calls=%async_computation.3 | async-start | bytes 65536 | tf_op jit(solution)/shard_map/all_to_all | solution.py:68
  533.6 22.9 %copy-start.101 = (f32[16,4,8,128]{3,2,0,1:T(8,128)S(1)}, f32[16,4,8,128]{3,2,0,1:T(8,128)}, u32[]{:S(2)}) copy-start(f32[16,4,8,128]{3,2,0,1:T(8,128)} %fusion.87) | copy-start | bytes 786436
  535.3 21.9 %copy-start.102 = (f32[16,4,8,128]{3,2,0,1:T(8,128)S(1)}, f32[16,4,8,128]{3,2,0,1:T(8,128)}, u32[]{:S(2)}) copy-start(f32[16,4,8,128]{3,2,0,1:T(8,128)} %fusion.89) | copy-start | bytes 786436
  535.4 21.9 %copy-start.104 = (f32[16,4,8,128]{3,2,0,1:T(8,128)S(1)}, f32[16,4,8,128]{3,2,0,1:T(8,128)}, u32[]{:S(2)}) copy-start(f32[16,4,8,128]{3,2,0,1:T(8,128)} %fusion.91) | copy-start | bytes 786436
  545.7 35.1 %all-to-all-start.1 = ((f32[64,1,32]{2,1,0:T(1,128)}), f32[64,1,32]{2,1,0:T(1,128)S(1)}, u32[]{:S(2)}, u32[]{:S(2)}) async-start(f32[64,1,32]{2,1,0:T(1,128)} %copy.800), calls=%async_computation.1 | async-start | bytes 65536 | tf_op jit(solution)/shard_map/all_to_all | solution.py:68
  580.8 34.0 %all-to-all-start.11 = ((f32[64,1,4096]{2,1,0:T(1,128)}), f32[64,1,4096]{2,1,0:T(1,128)}, u32[]{:S(2)}, u32[]{:S(2)}) async-start(f32[64,1,4096]{2,1,0:T(1,128)} %bitcast.538), calls=%async_computation.11 | async-start | bytes 2097152 | tf_op jit(solution)/shard_map/all_to_all | solution.py:67
  614.8 33.8 %all-to-all-start.10 = ((f32[64,1,4096]{2,1,0:T(1,128)}), f32[64,1,4096]{2,1,0:T(1,128)}, u32[]{:S(2)}, u32[]{:S(2)}) async-start(f32[64,1,4096]{2,1,0:T(1,128)} %bitcast.472), calls=%async_computation.10 | async-start | bytes 2097152 | tf_op jit(solution)/shard_map/all_to_all | solution.py:67
  648.7 33.9 %all-to-all-start.9 = ((f32[64,1,4096]{2,1,0:T(1,128)}), f32[64,1,4096]{2,1,0:T(1,128)}, u32[]{:S(2)}, u32[]{:S(2)}) async-start(f32[64,1,4096]{2,1,0:T(1,128)} %bitcast.406), calls=%async_computation.9 | async-start | bytes 2097152 | tf_op jit(solution)/shard_map/all_to_all | solution.py:67
  682.5 59.4 %all-to-all-start.8 = ((f32[64,1,4096]{2,1,0:T(1,128)}), f32[64,1,4096]{2,1,0:T(1,128)}, u32[]{:S(2)}, u32[]{:S(2)}) async-start(f32[64,1,4096]{2,1,0:T(1,128)} %bitcast.340), calls=%async_computation.8 | async-start | bytes 2097152 | tf_op jit(solution)/shard_map/all_to_all | solution.py:67
  691.9 159.6 %all-gather.2.cloned.1.call-start = ((), (), s32[]{:S(2)}) async-start(), calls=%async_computation.16 | async-start | bytes 2129920 | tf_op jit(solution)/shard_map/all_gather | solution.py:185
  694.9 46.2 %copy-start.225 = (f32[4,4,8]{2,0,1:T(4,128)S(1)}, f32[4,4,8]{2,0,1:T(4,128)}, u32[]{:S(2)}) copy-start(f32[4,4,8]{2,0,1:T(4,128)} %copy-done.224) | copy-start | bytes 1540
  694.9 46.4 %copy-start.227 = (f32[4,4,8]{2,0,1:T(4,128)S(1)}, f32[4,4,8]{2,0,1:T(4,128)}, u32[]{:S(2)}) copy-start(f32[4,4,8]{2,0,1:T(4,128)} %fusion.175) | copy-start | bytes 1540
  695.0 46.8 %copy-start.250 = (bf16[1,4,512]{2,1,0:T(4,128)(2,1)S(1)}, bf16[1,4,512]{2,1,0:T(4,128)(2,1)}, u32[]{:S(2)}) copy-start(bf16[1,4,512]{2,1,0:T(4,128)(2,1)} %param.12) | copy-start | bytes 12292
  (205 other events, 680.6 us)
Sparse Core Ops, SparseCore 0:
  746.8 104.7 all-gather.1
